TPU v7x, 512 devices: a whole 4x4x16 slice. The times are simulated.
512 devices in a mesh: lat: 4 (over y_hi, core), lon: 128 (over x, z, y_lo).
Axes of the slice: x: 4, y: 4 (y_hi: 2, y_lo: 2; y = y_hi * 2 + y_lo), z: 16, core: 2. Of those that a mesh axis runs over, the one named last changes fastest.
Arguments:
- features: bfloat16 [128, 1024, 1024], P('lat', 'lon'), may hold values from -18 to 18
- depth_kernel: bfloat16 [7, 7, 1024], replicated, may hold values from -0.875 to 0.875
- depth_bias: float32 [1024], replicated, may hold values from -3 to 3
- norm_gain: float32 [1024], replicated, may hold values from 0.1 to 1.9
- norm_bias: float32 [1024], replicated, may hold values from -3 to 3
- up_weight: bfloat16 [1024, 4096], P('lon', 'lat'), may hold values from -0.1875 to 0.1875
- up_bias: float32 [4096], P('lat'), may hold values from -3 to 3
- down_weight: bfloat16 [1024, 4096], P('lon', 'lat'), may hold values from -0.09375 to 0.09375
- down_bias: float32 [1024], replicated, may hold values from -3 to 3
- layer_scale: float32 [1024], replicated, may hold values from 0.3 to 2
Outputs:
- updated: bfloat16 [128, 1024, 1024], P('lat', 'lon')
All inputs are finite; a program needn't handle non-finite values.
Results may differ from a plain program's by a relative error of at most 0.0085.
Values may be sent and summed in bfloat16 or wider, within the bound.
A program may use at most 64 MiB of HBM per device.

v0:
```python
import jax
import jax.numpy as jnp
from jax import lax
from jax.sharding import PartitionSpec as P


def with_halo(block, sides, width, periodic):
    for axis, dim in sides:
        count = lax.axis_size(axis)
        forward = [(i, i + 1) for i in range(count - 1)]
        if periodic:
            forward.append((count - 1, 0))
        backward = [(target, source) for source, target in forward]
        low = lax.ppermute(
            lax.slice_in_dim(block, block.shape[dim] - width, None, axis=dim), axis, forward
        )
        high = lax.ppermute(lax.slice_in_dim(block, 0, width, axis=dim), axis, backward)
        block = jnp.concatenate([low, block, high], axis=dim)
    return block


def local(
    features,
    depth_kernel,
    depth_bias,
    norm_gain,
    norm_bias,
    up_weight,
    up_bias,
    down_weight,
    down_bias,
    layer_scale,
):
    row_count, col_count, chan_count = features.shape
    circled = with_halo(features, (("lon", 1),), 3, True)
    padded = with_halo(circled, (("lat", 0),), 3, False)
    kernel = depth_kernel.astype(jnp.float32)
    total = jnp.zeros((row_count, col_count, chan_count), jnp.float32) + depth_bias
    for row_off in range(7):
        for col_off in range(7):
            window = padded[row_off : row_off + row_count, col_off : col_off + col_count].astype(
                jnp.float32
            )
            total = total + window * kernel[row_off, col_off]
    centre = jnp.mean(total, axis=-1, keepdims=True)
    spread = jnp.mean((total - centre) ** 2, axis=-1, keepdims=True)
    normed = ((total - centre) * lax.rsqrt(spread + 1e-06) * norm_gain + norm_bias).astype(
        jnp.bfloat16
    )
    normed = normed.reshape(row_count * col_count, chan_count)
    gathered = lax.all_gather(normed, "lat", axis=0, tiled=True)
    pre = (
        jnp.dot(
            gathered,
            lax.all_gather(up_weight, "lon", axis=0, tiled=True),
            preferred_element_type=jnp.float32,
        )
        + up_bias
    )
    hidden = jax.nn.gelu(pre, approximate=False).astype(jnp.bfloat16)
    partial_out = lax.dot_general(
        hidden,
        lax.all_gather(down_weight, "lon", axis=0, tiled=True),
        (((1,), (1,)), ((), ())),
        preferred_element_type=jnp.float32,
    )
    branch = lax.psum_scatter(
        partial_out.astype(jnp.bfloat16), "lat", scatter_dimension=0, tiled=True
    ).astype(jnp.float32)
    branch = branch.reshape(row_count, col_count, chan_count)
    updated = features.astype(jnp.float32) + layer_scale * (branch + down_bias)
    return updated.astype(jnp.bfloat16)


def solution(mesh):
    placed = (
        P("lat", "lon", None),
        P(),
        P(),
        P(),
        P(),
        P("lon", "lat"),
        P("lat"),
        P("lon", "lat"),
        P(),
        P(),
    )
    return jax.shard_map(
        local, mesh=mesh, in_specs=placed, out_specs=P("lat", "lon", None), check_vma=False
    )
```

profile of v0, /device:TPU:1, one launch (start us, length us, event | category | flops | bytes accessed | tf_op | source)
XLA Modules:
  0.0 1329.8 jit_solution(5070489163931986096)
XLA Ops:
  6.5 0.0 copy-start
  6.5 0.0 all-gather.4.cloned.1.call-start
  6.5 1.5 fusion.79
  8.0 4.0 collective-permute-start
  12.0 13.0 collective-permute-start.1
  25.1 1.1 fusion.80
  26.3 1.2 fusion.81
  27.5 1.1 constant_dynamic-update-slice_fusion.1
  28.6 1.1 fusion.82
  29.7 0.0 collective-permute-done
  29.7 0.4 collective-permute-done.1
  30.1 0.0 copy-done
  30.1 0.1 pad_maximum_fusion.4
  30.2 6.0 collective-permute-start.2
  36.1 0.0 copy-start.1
  36.1 1.9 collective-permute-start.3
  38.1 0.2 constant_dynamic-update-slice_fusion
  38.3 0.0 collective-permute-done.2
  38.3 5.3 collective-permute-done.3
  43.6 0.7 maximum_maximum_fusion
  44.2 0.0 copy-done.1
  44.3 0.0 copy-start.2
  44.3 0.0 copy-start.3
  44.3 9.4 fusion.77
  53.7 0.0 copy-start.6
  53.7 0.3 multiply_reduce_fusion
  54.0 0.0 copy-done.2
  54.0 0.0 copy-done.3
  54.0 1.0 fusion.44
  55.1 0.0 all-gather.4.cloned.1.call-update
  55.1 0.0 all-gather.6.cloned.1.call-start
  55.1 0.7 all-gather.6.cloned.1.call-update
  55.8 0.0 all-gather.8.cloned.1.call-start
  55.9 0.7 all-gather.8.cloned.1.call-update
  56.6 0.0 reduce-scatter.2.cloned.1.call-start
  56.6 30.5 %all-gather.4.cloned.1.call-done = bf16[1024,1024]{1,0:T(8,128)(2,1)} async-done(((bf16[256,1024]{1,0:T(8,128)(2,1)}), bf16[1024,1024]{1,0:T(8,128)(2,1)}) %all-gather.4.cloned.1.call-update) | async-done | bytes 2097168 | tf_op jit(solution)/shard_map/all_gather | solution.py:51
  87.2 503.7 %all-gather.6.cloned.1.call-done = bf16[1024,1024]{1,0:T(8,128)(2,1)} async-done(((bf16[8,1024]{1,0:T(8,128)(2,1)}), bf16[1024,1024]{1,0:T(8,128)(2,1)}) %all-gather.6.cloned.1.call-update) | async-done | bytes 2097168 | tf_op jit(solution)/shard_map/all_gather | solution.py:55
  590.9 582.4 %all-gather.8.cloned.1.call-done = bf16[1024,1024]{1,0:T(8,128)(2,1)} async-done(((bf16[8,1024]{1,0:T(8,128)(2,1)}), bf16[1024,1024]{1,0:T(8,128)(2,1)}) %all-gather.8.cloned.1.call-update) | async-done | bytes 2097168 | tf_op jit(solution)/shard_map/all_gather | solution.py:63
  1173.3 0.0 copy-done.6
  1173.3 16.1 %fusion.14 = bf16[1024,1024]{1,0:T(8,128)(2,1)} fusion(bf16[1024,1024]{1,0:T(8,128)(2,1)} %all-gather.8.cloned.1.call-done, f32[1024]{0:T(1024)S(1)} %copy-done.6, bf16[1024,1024]{1,0:T(8,128)(2,1)} %all-gather.4.cloned.1.call-done, bf16[1024,1024]{1,0:T(8,128)(2,1)} %all-gather.6.cloned.1.call-done), kind=kOutput, calls=%fused_computation.21 | convolution fusion | flops 4365221888 | bytes 8392704 | tf_op jit(solution)/shard_map/dot_general | solution.py:61
  1189.4 0.0 copy-start.4
  1189.4 0.0 copy-start.5
  1189.4 0.0 reduce-scatter.2.cloned.1.call-update
  1189.5 131.8 %reduce-scatter.2.cloned.1.call-done = bf16[256,1024]{1,0:T(8,128)(2,1)} async-done(((bf16[1024,1024]{1,0:T(8,128)(2,1)}), bf16[256,1024]{1,0:T(8,128)(2,1)}) %reduce-scatter.2.cloned.1.call-update) | async-done | bytes 524304 | tf_op jit(solution)/shard_map/reduce_scatter | solution.py:67
  1321.2 0.0 copy-done.4
  1321.2 0.0 copy-done.5
  1321.2 2.0 fusion.42
  (2 shorter events, 0.0 us)
Async XLA Ops:
  6.5 23.5 %copy-start = (bf16[32,8,1024]{2,1,0:T(8,128)(2,1)S(1)}, bf16[32,8,1024]{2,1,0:T(8,128)(2,1)}, u32[]{:S(2)}) copy-start(bf16[32,8,1024]{2,1,0:T(8,128)(2,1)} %param.10) | copy-start | bytes 1572868
  6.5 80.6 %all-gather.4.cloned.1.call-start = ((), (), s32[]{:S(2)}) async-start(), calls=%async_computation.1 | async-start | bytes 2621440 | tf_op jit(solution)/shard_map/all_gather | solution.py:51
  8.0 21.7 %collective-permute-start = (bf16[32,3,1024]{2,1,0:T(4,128)(2,1)S(1)}, bf16[32,3,1024]{2,1,0:T(4,128)(2,1)S(1)}, u32[]{:S(2)}, u32[]{:S(2)}) collective-permute-start(bf16[32,3,1024]{2,1,0:T(4,128)(2,1)S(1)} %get-tuple-element.11), channel_id=1, source_target_pairs={{0,1},{1,2},{2,3},{3,4},{4,5},{5,6},{6,7},{7,8},{8,9},{9,10},{10,1... | collective-permute-start | bytes 589832 | tf_op jit(solution)/shard_map/ppermute | solution.py:14
  12.0 18.0 %collective-permute-start.1 = (bf16[32,3,1024]{2,1,0:T(4,128)(2,1)S(1)}, bf16[32,3,1024]{2,1,0:T(4,128)(2,1)S(1)}, u32[]{:S(2)}, u32[]{:S(2)}) collective-permute-start(bf16[32,3,1024]{2,1,0:T(4,128)(2,1)S(1)} %get-tuple-element.12), channel_id=1, source_target_pairs={{1,0},{2,1},{3,2},{4,3},{5,4},{6,5},{7,6},{8,7},{9,8},{10,9},{11,1... | collective-permute-start | bytes 589832 | tf_op jit(solution)/shard_map/ppermute | solution.py:17
  30.2 8.1 collective-permute-start.2
  36.1 8.1 copy-start.1
  36.1 7.4 collective-permute-start.3
  44.3 9.7 copy-start.2
  44.3 9.7 copy-start.3
  53.7 1119.6 %copy-start.6 = (f32[1024]{0:T(1024)S(1)}, f32[1024]{0:T(1024)}, u32[]{:S(2)}) copy-start(f32[1024]{0:T(1024)} %param.16) | copy-start | bytes 12292
  55.1 535.8 %all-gather.6.cloned.1.call-start = ((), (), s32[]{:S(2)}) async-start(), calls=%async_computation.2 | async-start | bytes 2113536 | tf_op jit(solution)/shard_map/all_gather | solution.py:55
  55.8 1117.5 %all-gather.8.cloned.1.call-start = ((), (), s32[]{:S(2)}) async-start(), calls=%async_computation.3 | async-start | bytes 2113536 | tf_op jit(solution)/shard_map/all_gather | solution.py:63
  56.6 1264.7 %reduce-scatter.2.cloned.1.call-start = ((), (), s32[]{:S(2)}) async-start(), calls=%async_computation.4 | async-start | bytes 2621440 | tf_op jit(solution)/shard_map/reduce_scatter | solution.py:67
  1189.4 131.8 %copy-start.4 = (f32[1024]{0:T(1024)S(1)}, f32[1024]{0:T(1024)}, u32[]{:S(2)}) copy-start(f32[1024]{0:T(1024)} %param.18) | copy-start | bytes 12292
  1189.4 131.8 %copy-start.5 = (f32[1024]{0:T(1024)S(1)}, f32[1024]{0:T(1024)}, u32[]{:S(2)}) copy-start(f32[1024]{0:T(1024)} %param.19) | copy-start | bytes 12292
Sparse Core Ops, SparseCore 0:
  55.2 31.9 all-gather.3
  89.2 501.5 all-gather.5
  592.9 580.2 all-gather.7
  1189.6 131.5 reduce-scatter.1
where the time goes:
time: 1330 us
  waiting for transfers between devices  1260 us (95%)
  starting transfers between devices  25.1 us (2%)
  matrix products  16.1 us (1%)
  other arithmetic  13.5 us (1%)
  between operations  13.3 us (1%)
    all_gather x1, waiting for transfers between devices, local(): lax.all_gather(down_weight, 'lon', axis=0, tiled=True)  582 us
    all_gather x1, waiting for transfers between devices, local(): lax.all_gather(up_weight, 'lon', axis=0, tiled=True)  504 us
    reduce_scatter x1, waiting for transfers between devices, local(): lax.psum_scatter(partial_out.astype(jnp.bfloat16), 'lat', scatter_dimensi...  132 us
    all_gather x1, waiting for transfers between devices, local(): gathered = lax.all_gather(normed, 'lat', axis=0, tiled=True)  30.5 us
  transfers between devices with their start and end apart: 8, of which 6 were waited for; matrix products, arithmetic and copies ran while one was open for 0% of the time, Pallas kernels for 0%

commit v1 on v0

--- a/solution.py
+++ b/solution.py
@@ -60,7 +60,9 @@
     hidden = jax.nn.gelu(pre, approximate=False).astype(jnp.bfloat16)
     partial_out = lax.dot_general(
         hidden,
-        lax.all_gather(down_weight, "lon", axis=0, tiled=True),
+        jnp.concatenate(
+            lax.all_to_all(jnp.stack([down_weight] * lax.axis_size("lon")), "lon", 0, 0), axis=0
+        ),
         (((1,), (1,)), ((), ())),
         preferred_element_type=jnp.float32,
     )

time: 1330 us -> 762 us (0.57)
  waiting for transfers between devices: 1260 us -> 678 us
    all_gather x1 -> x0, waiting for transfers between devices: 582 us -> none  [local(): lax.all_gather(down_weight, 'lon', axis=0, tiled=True)]
  transfers between devices with their start and end apart: 8 -> 8, of which waited for: 6 -> 4; matrix products, arithmetic and copies ran while one was open for 0% -> 2% of each run, Pallas kernels for 0% -> 0%
where the time goes in v1:
time: 762 us; the launch traced here: 761 us
  waiting for transfers between devices  678 us (89%)
  starting transfers between devices  36.3 us (5%)
  matrix products  15.5 us (2%)
  other arithmetic  13.5 us (2%)
  between operations  13.3 us (2%)
    all_gather x1, waiting for transfers between devices, local(): lax.all_gather(up_weight, 'lon', axis=0, tiled=True)  505 us
    reduce_scatter x1, waiting for transfers between devices, local(): lax.psum_scatter(partial_out.astype(jnp.bfloat16), 'lat', scatter_dimensi...  131 us
    all_gather x1, waiting for transfers between devices, local(): gathered = lax.all_gather(normed, 'lat', axis=0, tiled=True)  35.2 us
    dot_general x1, matrix products, local(): lax.dot_general(hidden, jnp.concatenate(lax.all_to_all(jnp.stack([down_we...  15.5 us
  transfers between devices with their start and end apart: 8, of which 4 were waited for; matrix products, arithmetic and copies ran while one was open for 2% of the time, Pallas kernels for 0%

profile of v1, /device:TPU:1, one launch (start us, length us, event | category | flops | bytes accessed | tf_op | source)
XLA Modules:
  0.0 761.1 jit_solution(5168302659967119073)
XLA Ops:
  6.5 2.1 fusion.112
  8.7 4.0 collective-permute-start
  12.7 13.0 %collective-permute-start.1 = (bf16[32,3,1024]{2,1,0:T(4,128)(2,1)S(1)}, bf16[32,3,1024]{2,1,0:T(4,128)(2,1)S(1)}, u32[]{:S(2)}, u32[]{:S(2)}) collective-permute-start(bf16[32,3,1024]{2,1,0:T(4,128)(2,1)S(1)} %get-tuple-element.12), channel_id=1, source_target_pairs={{1,0},{2,1},{3,2},{4,3},{5,4},{6,5},{7,6},{8,7},{9,8},{10,9},{11,1... | collective-permute-start | bytes 589832 | tf_op jit(solution)/shard_map/ppermute | solution.py:17
  25.8 2.3 stack.2
  28.1 0.0 copy-start.1
  28.1 0.0 copy-start
  28.1 10.8 %all-to-all-start = ((bf16[128,8,1024]{2,1,0:T(8,128)(2,1)}), bf16[128,8,1024]{2,1,0:T(8,128)(2,1)S(1)}, u32[]{:S(2)}, u32[]{:S(2)}) async-start(bf16[128,8,1024]{2,1,0:T(8,128)(2,1)} %stack.2), calls=%async_computation | async-start | bytes 4194304 | tf_op jit(solution)/shard_map/all_to_all | solution.py:64
  38.9 0.0 all-gather.3.cloned.1.call-start
  38.9 0.0 copy-done.1
  38.9 0.1 fusion.113
  39.0 0.1 fusion.114
  39.1 0.0 copy-done
  39.2 0.0 collective-permute-done
  39.2 0.0 collective-permute-done.1
  39.2 0.1 pad_maximum_fusion.4
  39.3 6.2 collective-permute-start.2
  45.5 0.0 copy-start.2
  45.5 1.9 collective-permute-start.3
  47.5 0.2 constant_dynamic-update-slice_fusion
  47.6 0.0 collective-permute-done.2
  47.7 5.7 collective-permute-done.3
  53.3 0.6 maximum_maximum_fusion
  54.0 0.0 copy-done.2
  54.0 0.0 copy-start.3
  54.0 0.0 copy-start.4
  54.0 9.4 %fusion.110 = (f32[32,8]{1,0:T(8,128)S(1)}, f32[32,8,1024]{2,1,0:T(8,128)S(1)}) fusion(f32[1024]{0:T(1024)S(1)} %bitcast.109, bf16[35,14,1024]{2,1,0:T(8,128)(2,1)S(1)} %get-tuple-element.8, f32[1024]{0:T(1024)S(1)} %bitcast.108, f32[1024]{0:T(1024)S(1)} %bitcast.107, f32[1024]{0:T(1024)S(1)} %bitcast.106, f32[1024]{0:T(1024)S(1)} %bitcast.105, ...), kind=kLoop, calls=%fused_computation.132 | loop fusion | flops 41156352 | bytes 25568256 | tf_op jit(solution)/shard_map/reduce_sum | solution.py:45
  63.5 0.0 copy-start.7
  63.5 0.3 multiply_reduce_fusion
  63.7 0.0 copy-done.3
  63.7 0.0 copy-done.4
  63.8 1.0 fusion.77
  64.8 0.0 all-gather.3.cloned.1.call-update
  64.8 0.0 all-gather.5.cloned.1.call-start
  64.9 0.7 all-gather.5.cloned.1.call-update
  65.6 0.2 reduce-scatter.2.cloned.1.call-start
  65.8 35.2 %all-gather.3.cloned.1.call-done = bf16[1024,1024]{1,0:T(8,128)(2,1)} async-done(((bf16[256,1024]{1,0:T(8,128)(2,1)}), bf16[1024,1024]{1,0:T(8,128)(2,1)}) %all-gather.3.cloned.1.call-update) | async-done | bytes 2097168 | tf_op jit(solution)/shard_map/all_gather | solution.py:51
  101.0 505.3 %all-gather.5.cloned.1.call-done = bf16[1024,1024]{1,0:T(8,128)(2,1)} async-done(((bf16[8,1024]{1,0:T(8,128)(2,1)}), bf16[1024,1024]{1,0:T(8,128)(2,1)}) %all-gather.5.cloned.1.call-update) | async-done | bytes 2097168 | tf_op jit(solution)/shard_map/all_gather | solution.py:55
  606.3 0.0 all-to-all-done
  606.3 0.0 copy-done.7
  606.3 15.5 %fusion.45 = bf16[1024,1024]{1,0:T(8,128)(2,1)} fusion(bf16[128,8,1024]{2,1,0:T(8,128)(2,1)S(1)} %all-to-all-done, f32[1024]{0:T(1024)S(1)} %copy-done.7, bf16[1024,1024]{1,0:T(8,128)(2,1)} %all-gather.3.cloned.1.call-done, bf16[1024,1024]{1,0:T(8,128)(2,1)} %all-gather.5.cloned.1.call-done), kind=kOutput, calls=%fused_computation.52 | convolution fusion | flops 4365221888 | bytes 8392704 | tf_op jit(solution)/shard_map/dot_general | solution.py:61
  621.9 0.0 copy-start.5
  621.9 0.0 copy-start.6
  621.9 0.0 reduce-scatter.2.cloned.1.call-update
  621.9 130.6 %reduce-scatter.2.cloned.1.call-done = bf16[256,1024]{1,0:T(8,128)(2,1)} async-done(((bf16[1024,1024]{1,0:T(8,128)(2,1)}), bf16[256,1024]{1,0:T(8,128)(2,1)}) %reduce-scatter.2.cloned.1.call-update) | async-done | bytes 524304 | tf_op jit(solution)/shard_map/reduce_scatter | solution.py:69
  752.5 0.0 copy-done.5
  752.5 0.0 copy-done.6
  752.5 2.0 fusion.75
  (4 shorter events, 0.1 us)
Async XLA Ops:
  8.7 30.5 %collective-permute-start = (bf16[32,3,1024]{2,1,0:T(4,128)(2,1)}, bf16[32,3,1024]{2,1,0:T(4,128)(2,1)S(1)}, u32[]{:S(2)}, u32[]{:S(2)}) collective-permute-start(bf16[32,3,1024]{2,1,0:T(4,128)(2,1)} %get-tuple-element.11), channel_id=1, source_target_pairs={{0,1},{1,2},{2,3},{3,4},{4,5},{5,6},{6,7},{7,8},{8,9},{9,10},{10,1... | collective-permute-start | bytes 589832 | tf_op jit(solution)/shard_map/ppermute | solution.py:14
  12.7 26.5 %collective-permute-start.1 = (bf16[32,3,1024]{2,1,0:T(4,128)(2,1)S(1)}, bf16[32,3,1024]{2,1,0:T(4,128)(2,1)S(1)}, u32[]{:S(2)}, u32[]{:S(2)}) collective-permute-start(bf16[32,3,1024]{2,1,0:T(4,128)(2,1)S(1)} %get-tuple-element.12), channel_id=1, source_target_pairs={{1,0},{2,1},{3,2},{4,3},{5,4},{6,5},{7,6},{8,7},{9,8},{10,9},{11,1... | collective-permute-start | bytes 589832 | tf_op jit(solution)/shard_map/ppermute | solution.py:17
  28.1 10.8 %copy-start.1 = (bf16[7,7,1024]{2,1,0:T(8,128)(2,1)S(1)}, bf16[7,7,1024]{2,1,0:T(8,128)(2,1)}, u32[]{:S(2)}) copy-start(bf16[7,7,1024]{2,1,0:T(8,128)(2,1)} %param.11) | copy-start | bytes 301060
  28.1 11.0 %copy-start = (bf16[32,8,1024]{2,1,0:T(8,128)(2,1)S(1)}, bf16[32,8,1024]{2,1,0:T(8,128)(2,1)}, u32[]{:S(2)}) copy-start(bf16[32,8,1024]{2,1,0:T(8,128)(2,1)} %param.10) | copy-start | bytes 1572868
  28.1 578.2 %all-to-all-start = ((bf16[128,8,1024]{2,1,0:T(8,128)(2,1)}), bf16[128,8,1024]{2,1,0:T(8,128)(2,1)S(1)}, u32[]{:S(2)}, u32[]{:S(2)}) async-start(bf16[128,8,1024]{2,1,0:T(8,128)(2,1)} %stack.2), calls=%async_computation | async-start | bytes 4194304 | tf_op jit(solution)/shard_map/all_to_all | solution.py:64
  38.9 62.2 %all-gather.3.cloned.1.call-start = ((), (), s32[]{:S(2)}) async-start(), calls=%async_computation.2 | async-start | bytes 2621440 | tf_op jit(solution)/shard_map/all_gather | solution.py:51
  39.3 8.4 %collective-permute-start.2 = (bf16[3,14,1024]{2,1,0:T(8,128)(2,1)S(1)}, bf16[3,14,1024]{2,1,0:T(8,128)(2,1)S(1)}, u32[]{:S(2)}, u32[]{:S(2)}) collective-permute-start(bf16[3,14,1024]{2,1,0:T(8,128)(2,1)S(1)} %get-tuple-element.9), channel_id=1, source_target_pairs={{0,128},{128,256},{256,384},{1,129},{129,257},{257,385},{2,130},{1... | collective-permute-start | bytes 258056 | tf_op jit(solution)/shard_map/ppermute | solution.py:14
  45.5 8.5 %copy-start.2 = (f32[1024]{0:T(1024)S(1)}, f32[1024]{0:T(1024)}, u32[]{:S(2)}) copy-start(f32[1024]{0:T(1024)} %param.12) | copy-start | bytes 12292
  45.5 7.8 %collective-permute-start.3 = (bf16[3,14,1024]{2,1,0:T(8,128)(2,1)S(1)}, bf16[3,14,1024]{2,1,0:T(8,128)(2,1)S(1)}, u32[]{:S(2)}, u32[]{:S(2)}) collective-permute-start(bf16[3,14,1024]{2,1,0:T(8,128)(2,1)S(1)} %get-tuple-element.10), channel_id=1, source_target_pairs={{128,0},{256,128},{384,256},{129,1},{257,129},{385,257},{130,2},{2... | collective-permute-start | bytes 258056 | tf_op jit(solution)/shard_map/ppermute | solution.py:17
  54.0 9.7 %copy-start.3 = (f32[1024]{0:T(1024)S(1)}, f32[1024]{0:T(1024)}, u32[]{:S(2)}) copy-start(f32[1024]{0:T(1024)} %param.14) | copy-start | bytes 12292
  54.0 9.7 %copy-start.4 = (f32[1024]{0:T(1024)S(1)}, f32[1024]{0:T(1024)}, u32[]{:S(2)}) copy-start(f32[1024]{0:T(1024)} %param.13) | copy-start | bytes 12292
  63.5 542.9 %copy-start.7 = (f32[1024]{0:T(1024)S(1)}, f32[1024]{0:T(1024)}, u32[]{:S(2)}) copy-start(f32[1024]{0:T(1024)} %param.16) | copy-start | bytes 12292
  64.8 541.5 %all-gather.5.cloned.1.call-start = ((), (), s32[]{:S(2)}) async-start(), calls=%async_computation.3 | async-start | bytes 2113536 | tf_op jit(solution)/shard_map/all_gather | solution.py:55
  65.6 686.9 %reduce-scatter.2.cloned.1.call-start = ((), (), s32[]{:S(2)}) async-start(), calls=%async_computation.4 | async-start | bytes 2621440 | tf_op jit(solution)/shard_map/reduce_scatter | solution.py:69
  621.9 130.6 %copy-start.5 = (f32[1024]{0:T(1024)S(1)}, f32[1024]{0:T(1024)}, u32[]{:S(2)}) copy-start(f32[1024]{0:T(1024)} %param.18) | copy-start | bytes 12292
  621.9 130.6 %copy-start.6 = (f32[1024]{0:T(1024)S(1)}, f32[1024]{0:T(1024)}, u32[]{:S(2)}) copy-start(f32[1024]{0:T(1024)} %param.19) | copy-start | bytes 12292
Sparse Core Ops, SparseCore 0:
  64.9 36.0 all-gather.2
  103.1 503.1 all-gather.4
  622.0 130.4 reduce-scatter.1
